TPU v7x, 128 devices: a whole 4x4x4 slice. The times are simulated.
128 devices in a mesh: ra: 16 (over x, y_hi, core), dec: 8 (over z, y_lo).
Axes of the slice: x: 4, y: 4 (y_hi: 2, y_lo: 2; y = y_hi * 2 + y_lo), z: 4, core: 2. Of those that a mesh axis runs over, the one named last changes fastest.
Arguments:
- log_flux: float32 [5, 32768], P(None, ('ra', 'dec')), may hold values from 5.5 to 9.5
- position: float32 [2, 32768], P(None, ('ra', 'dec')), may hold values from 0 to 640
- log_width: float32 [32768], P(('ra', 'dec')), may hold values from -3.5 to -0.5
- owner_tile: int32 [32768, 1], P(('ra', 'dec')), may hold values from 0 to 127; in each aligned block of 256 rows (0 to 255, 256 to 511, ...) at most 4 rows name the same one
- sky_level: float32 [16, 8, 5], P('ra', 'dec'), may hold values from 0.5 to 4
- counts: int32 [5, 10240, 5120], P(None, 'ra', 'dec'), may hold values from 0 to 7
Outputs:
- gradient: float32 [8, 32768], P(None, ('ra', 'dec'))
Inputs may be any that keep to these rules, and one draw needn't show every extreme that they name: `owner_tile`: in each aligned block of 256 catalog rows (the rows of one device) no tile is named more than 4 times, a bound that some block reaches.
All inputs are finite; a program needn't handle non-finite values.
Results may differ from a plain program's by a relative error of at most 0.00095.
Values may be sent and summed in bfloat16 or wider, within the bound.
A program may use at most 128 MiB of HBM per device.

v0:
```python
import math
import jax
import jax.numpy as jnp
from jax import lax
from jax.sharding import PartitionSpec as P

MARGIN = 128
CAT_DEV = 256


def passed_along(value, axis, steps):
    count = lax.axis_size(axis)
    leading, last = (max(0, -steps), min(count, count - steps))
    return lax.ppermute(value, axis, [(source, source + steps) for source in range(leading, last)])


def with_halo(cells, sides, width):
    for axis, dim in sides:
        count = lax.axis_size(axis)
        ends = count - 1
        head = lax.slice_in_dim(cells, 0, width, axis=dim)
        tail = lax.slice_in_dim(cells, cells.shape[dim] - width, cells.shape[dim], axis=dim)
        cells = jnp.concatenate(
            [
                lax.ppermute(tail, axis, [(i, (i + 1) % count) for i in range(ends)]),
                cells,
                lax.ppermute(head, axis, [((i + 1) % count, i) for i in range(ends)]),
            ],
            axis=dim,
        )
    return cells


def profiles(center, log_width, length):
    coords = jnp.arange(length, dtype=jnp.float32) - MARGIN + 0.5
    sigma = MARGIN * jnp.exp(log_width)
    offset = (coords[:, None] - center[None, :]) / sigma[None, :]
    shape = jnp.exp(-0.5 * offset * offset) / (math.sqrt(2.0 * math.pi) * sigma[None, :])
    return (shape, offset, sigma)


def on_device(log_flux, position, log_width, owner_tile, sky_level, counts):
    tile_count = lax.axis_size("ra") * lax.axis_size("dec")
    capacity = max(2, 2 * CAT_DEV // tile_count)
    slot_count = tile_count * capacity
    tile_side = counts.shape[1]
    canvas_side = tile_side + 2 * MARGIN
    rows_here = log_flux.shape[1]
    target_tile = owner_tile[:, 0]
    order = jnp.arange(rows_here, dtype=jnp.int32)
    matches = (target_tile[:, None] == target_tile[None, :]) & (order[None, :] < order[:, None])
    rank_in = jnp.sum(matches.astype(jnp.int32), axis=1)
    target_slot = target_tile * capacity + rank_in
    onehot = (target_slot[:, None] == jnp.arange(slot_count, dtype=jnp.int32)[None, :]).astype(
        jnp.float32
    )
    params = jnp.concatenate(
        [log_flux, position, log_width[None, :], jnp.ones((1, rows_here), jnp.float32)], axis=0
    )
    outgoing = jnp.dot(params, onehot, precision=lax.Precision.HIGHEST)
    arrived = lax.all_to_all(outgoing, ("ra", "dec"), split_axis=1, concat_axis=1, tiled=True)
    flux_values = arrived[8][None, :] * jnp.exp(arrived[0:5])
    row_prof, row_off, sigma = profiles(arrived[5], arrived[7], canvas_side)
    col_prof, col_off, _ = profiles(arrived[6], arrived[7], canvas_side)
    row_bf = row_prof.astype(jnp.bfloat16)
    col_bf = col_prof.astype(jnp.bfloat16)
    scaled = (row_prof[None, :, :] * flux_values[:, None, :]).astype(jnp.bfloat16)
    canvas = jnp.einsum("bis,js->bij", scaled, col_bf, preferred_element_type=jnp.float32).astype(
        jnp.bfloat16
    )
    edge = MARGIN
    inner_end = edge + tile_side
    rim_start = tile_side - edge
    interior = canvas[:, edge:inner_end, edge:inner_end].astype(jnp.float32)
    from_below = passed_along(canvas[:, :edge, edge:inner_end], "ra", -1)
    from_above = passed_along(canvas[:, inner_end:, edge:inner_end], "ra", 1)
    from_right = passed_along(canvas[:, edge:inner_end, :edge], "dec", -1)
    from_left = passed_along(canvas[:, edge:inner_end, inner_end:], "dec", 1)
    interior = interior.at[:, rim_start:, :].add(from_below.astype(jnp.float32))
    interior = interior.at[:, :edge, :].add(from_above.astype(jnp.float32))
    interior = interior.at[:, :, rim_start:].add(from_right.astype(jnp.float32))
    interior = interior.at[:, :, :edge].add(from_left.astype(jnp.float32))
    upper_pair = jnp.concatenate([canvas[:, :edge, :edge], canvas[:, :edge, inner_end:]], axis=2)
    lower_pair = jnp.concatenate(
        [canvas[:, inner_end:, :edge], canvas[:, inner_end:, inner_end:]], axis=2
    )
    below_pair = passed_along(upper_pair, "ra", -1)
    above_pair = passed_along(lower_pair, "ra", 1)
    leftward = jnp.concatenate([below_pair[:, :, :edge], above_pair[:, :, :edge]], axis=1)
    rightward = jnp.concatenate([below_pair[:, :, edge:], above_pair[:, :, edge:]], axis=1)
    got_left = passed_along(leftward, "dec", -1).astype(jnp.float32)
    got_right = passed_along(rightward, "dec", 1).astype(jnp.float32)
    interior = interior.at[:, rim_start:, rim_start:].add(got_left[:, :edge])
    interior = interior.at[:, :edge, rim_start:].add(got_left[:, edge:])
    interior = interior.at[:, rim_start:, :edge].add(got_right[:, :edge])
    interior = interior.at[:, :edge, :edge].add(got_right[:, edge:])
    intensity = sky_level.reshape(-1)[:, None, None] + interior
    weights = (counts.astype(jnp.float32) / intensity - 1.0).astype(jnp.bfloat16)
    weight_canvas = with_halo(weights, (("ra", 1), ("dec", 2)), MARGIN)
    along_rows = jnp.einsum(
        "bij,js->bis", weight_canvas, col_bf, preferred_element_type=jnp.float32
    )
    along_cols = jnp.einsum(
        "bij,is->bjs", weight_canvas, row_bf, preferred_element_type=jnp.float32
    )
    flux_grad = flux_values * jnp.sum(row_bf.astype(jnp.float32)[None, :, :] * along_rows, axis=1)
    row_total = jnp.sum(flux_values[:, None, :] * along_rows, axis=0)
    col_total = jnp.sum(flux_values[:, None, :] * along_cols, axis=0)
    row_grad = jnp.sum(row_prof * row_off / sigma[None, :] * row_total, axis=0)
    col_grad = jnp.sum(col_prof * col_off / sigma[None, :] * col_total, axis=0)
    width_grad = jnp.sum(row_prof * (row_off * row_off - 1.0) * row_total, axis=0) + jnp.sum(
        col_prof * (col_off * col_off - 1.0) * col_total, axis=0
    )
    slot_grad = jnp.concatenate(
        [flux_grad, row_grad[None], col_grad[None], width_grad[None]], axis=0
    )
    returned = lax.all_to_all(slot_grad, ("ra", "dec"), split_axis=1, concat_axis=1, tiled=True)
    return jnp.dot(returned, onehot.T, precision=lax.Precision.HIGHEST)


def solution(mesh):
    in_specs = (
        P(None, ("ra", "dec")),
        P(None, ("ra", "dec")),
        P(("ra", "dec")),
        P(("ra", "dec"), None),
        P("ra", "dec", None),
        P(None, "ra", "dec"),
    )
    out_specs = P(None, ("ra", "dec"))
    return jax.shard_map(
        on_device, mesh=mesh, in_specs=in_specs, out_specs=out_specs, check_vma=False
    )
```

profile of v0, /device:TPU:1, one launch (start us, length us, event | category | flops | bytes accessed | tf_op | source)
XLA Modules:
  0.0 254.1 jit_solution(15445283636594914386)
XLA Ops:
  1.7 2.1 fusion.21
  3.8 11.5 %all-to-all-start = ((f32[9,128,4]{0,2,1:T(4,128)}), f32[9,128,4]{0,2,1:T(4,128)S(1)}, u32[]{:S(2)}, u32[]{:S(2)}) async-start(f32[9,128,4]{0,2,1:T(4,128)} %bitcast.4), calls=%async_computation | async-start | bytes 524288 | tf_op jit(solution)/shard_map/all_to_all | solution.py:61
  17.4 10.3 %copy.91 = s32[5,640,640]{1,2,0:T(8,128)} copy(s32[5,640,640]{2,1,0:T(8,128)} %param.27) | data formatting | bytes 16384000 | tf_op args[5]
  30.5 5.1 %convolution_convert_fusion = bf16[5,896,896]{1,2,0:T(8,128)(2,1)S(1)} fusion(f32[5,512]{1,0:T(8,128)S(1)} %broadcast_multiply_fusion, f32[896,512]{1,0:T(8,128)S(1)} %get-tuple-element.132, f32[512]{0:T(512)S(1)} %mul.154, f32[512]{0:T(512)S(1)} %mul.149, f32[512]{0:T(512)S(1)} %sub.53, f32[896]{0:T(1024)S(1)} %iota_add_fusion), kind=kOutput, calls=%fused_computation.6 | convolution fusion | flops 4121772032 | bytes 9883136 | tf_op jit(solution)/shard_map/bis,js->bij/dot_general | solution.py:68
  36.1 5.1 %collective-permute-start.5 = (bf16[5,128,256]{1,2,0:T(8,128)(2,1)S(1)}, bf16[5,128,256]{1,2,0:T(8,128)(2,1)S(1)}, u32[]{:S(2)}, u32[]{:S(2)}) collective-permute-start(bf16[5,128,256]{1,2,0:T(8,128)(2,1)S(1)} %pad_maximum_fusion.5), channel_id=1, source_target_pairs={{0,8},{8,16},{16,24},{24,32},{32,40},{40,48},{48,56},{56,64},{64,7... | collective-permute-start | bytes 983048 | tf_op jit(solution)/shard_map/ppermute | solution.py:14
  41.2 1.9 collective-permute-start.4
  43.3 5.1 %collective-permute-start.1 = (bf16[5,128,640]{1,2,0:T(8,128)(2,1)S(1)}, bf16[5,128,640]{1,2,0:T(8,128)(2,1)S(1)}, u32[]{:S(2)}, u32[]{:S(2)}) collective-permute-start(bf16[5,128,640]{1,2,0:T(8,128)(2,1)S(1)} %get-tuple-element.120), channel_id=1, source_target_pairs={{0,8},{8,16},{16,24},{24,32},{32,40},{40,48},{48,56},{56,64},{64,7... | collective-permute-start | bytes 2457608 | tf_op jit(solution)/shard_map/ppermute | solution.py:14
  53.2 4.6 %collective-permute-start.7 = (bf16[5,256,128]{1,2,0:T(8,128)(2,1)S(1)}, bf16[5,256,128]{1,2,0:T(8,128)(2,1)S(1)}, u32[]{:S(2)}, u32[]{:S(2)}) collective-permute-start(bf16[5,256,128]{1,2,0:T(8,128)(2,1)S(1)} %pad_maximum_fusion.7), channel_id=1, source_target_pairs={{0,1},{1,2},{2,3},{3,4},{4,5},{5,6},{6,7},{8,9},{9,10},{10,11},{11... | collective-permute-start | bytes 983048 | tf_op jit(solution)/shard_map/ppermute | solution.py:14
  58.4 43.4 %collective-permute-done.6 = bf16[5,256,128]{1,2,0:T(8,128)(2,1)S(1)} collective-permute-done((bf16[5,256,128]{1,2,0:T(8,128)(2,1)S(1)}, bf16[5,256,128]{1,2,0:T(8,128)(2,1)S(1)}, u32[]{:S(2)}, u32[]{:S(2)}) %collective-permute-start.6) | collective-permute-done | bytes 327712 | tf_op jit(solution)/shard_map/ppermute | solution.py:14
  101.8 3.6 %collective-permute-start.3 = (bf16[5,640,128]{1,2,0:T(8,128)(2,1)S(1)}, bf16[5,640,128]{1,2,0:T(8,128)(2,1)S(1)}, u32[]{:S(2)}, u32[]{:S(2)}) collective-permute-start(bf16[5,640,128]{1,2,0:T(8,128)(2,1)S(1)} %get-tuple-element.118), channel_id=1, source_target_pairs={{0,1},{1,2},{2,3},{3,4},{4,5},{5,6},{6,7},{8,9},{9,10},{10,11},{11... | collective-permute-start | bytes 2457608 | tf_op jit(solution)/shard_map/ppermute | solution.py:14
  106.6 7.9 %collective-permute-done.3 = bf16[5,640,128]{1,2,0:T(8,128)(2,1)S(1)} collective-permute-done((bf16[5,640,128]{1,2,0:T(8,128)(2,1)S(1)}, bf16[5,640,128]{1,2,0:T(8,128)(2,1)S(1)}, u32[]{:S(2)}, u32[]{:S(2)}) %collective-permute-start.3) | collective-permute-done | bytes 819232 | tf_op jit(solution)/shard_map/ppermute | solution.py:14
  114.9 3.2 %copy-done = f32[5,640,640]{1,2,0:T(8,128)} copy-done((f32[5,640,640]{1,2,0:T(8,128)}, f32[5,640,640]{1,2,0:T(8,128)S(1)}, u32[]{:S(2)}) %copy-start) | copy-done | bytes 8192024
  118.1 2.1 add_select_fusion
  120.2 5.8 %scatter-add.35 = f32[5,640,640]{1,2,0:T(8,128)} dynamic-update-slice(f32[5,640,640]{1,2,0:T(8,128)} %copy-done, f32[5,128,128]{1,2,0:T(8,128)S(1)} %add_select_fusion, s32[]{:T(128)} %constant.235.clone.1, s32[]{:T(128)} %bitcast.8, s32[]{:T(128)} %bitcast.9) | dynamic-update-slice | bytes 655364 | tf_op jit(solution)/shard_map/scatter-add | solution.py:94
  129.5 7.3 %add_convert_fusion = bf16[5,640,640]{1,2,0:T(8,128)(2,1)S(1)} fusion(f32[5,640,640]{1,2,0:T(8,128)} %fusion.22, s32[5,640,640]{1,2,0:T(8,128)} %copy.91, f32[5]{0:T(128)S(1)} %bitcast.31), kind=kLoop, calls=%fused_computation.4 | loop fusion | flops 10240000 | bytes 20480020 | tf_op jit(solution)/shard_map/convert_element_type | solution.py:98
  139.1 2.5 collective-permute-start.9
  141.5 20.7 %collective-permute-done.8 = bf16[5,128,640]{1,2,0:T(8,128)(2,1)S(1)} collective-permute-done((bf16[5,128,640]{1,2,0:T(8,128)(2,1)S(1)}, bf16[5,128,640]{1,2,0:T(8,128)(2,1)S(1)}, u32[]{:S(2)}, u32[]{:S(2)}) %collective-permute-start.8) | collective-permute-done | bytes 819232 | tf_op jit(solution)/shard_map/ppermute | solution.py:25
  164.2 6.1 %collective-permute-start.10 = (bf16[5,896,128]{1,2,0:T(8,128)(2,1)}, bf16[5,896,128]{1,2,0:T(8,128)(2,1)}, u32[]{:S(2)}, u32[]{:S(2)}) collective-permute-start(bf16[5,896,128]{1,2,0:T(8,128)(2,1)} %get-tuple-element.122), channel_id=1, source_target_pairs={{0,1},{1,2},{2,3},{3,4},{4,5},{5,6},{6,7},{8,9},{9,10},{10,11},{11... | collective-permute-start | bytes 3440648 | tf_op jit(solution)/shard_map/ppermute | solution.py:25
  171.7 10.6 %collective-permute-done.10 = bf16[5,896,128]{1,2,0:T(8,128)(2,1)} collective-permute-done((bf16[5,896,128]{1,2,0:T(8,128)(2,1)}, bf16[5,896,128]{1,2,0:T(8,128)(2,1)}, u32[]{:S(2)}, u32[]{:S(2)}) %collective-permute-start.10) | collective-permute-done | bytes 1146912 | tf_op jit(solution)/shard_map/ppermute | solution.py:25
  182.3 27.7 %collective-permute-done.11 = bf16[5,896,128]{1,2,0:T(8,128)(2,1)} collective-permute-done((bf16[5,896,128]{1,2,0:T(8,128)(2,1)}, bf16[5,896,128]{1,2,0:T(8,128)(2,1)}, u32[]{:S(2)}, u32[]{:S(2)}) %collective-permute-start.11) | collective-permute-done | bytes 1146912 | tf_op jit(solution)/shard_map/ppermute | solution.py:27
  210.0 9.9 %multiply_reduce_fusion = f32[896,512]{1,0:T(8,128)S(1)} fusion(f32[5,512]{1,0:T(8,128)S(1)} %broadcast_multiply_fusion, f32[512]{0:T(512)S(1)} %mul.154, f32[512]{0:T(512)S(1)} %mul.149, f32[512]{0:T(512)S(1)} %sub.50, f32[896]{0:T(1024)S(1)} %iota_add_fusion, bf16[5,896,128]{1,2,0:T(8,128)(2,1)} %collective-permute-done.11, ...), kind=kOutput, calls=%fused_computation | convolution fusion | flops 4157440000 | bytes 9883136 | tf_op jit(solution)/shard_map/bij,is->bjs/dot_general | solution.py:103
  220.0 7.7 %multiply_reduce_fusion.2 = (f32[5,512]{1,0:T(8,128)S(1)}, f32[896,512]{1,0:T(8,128)S(1)}) fusion(f32[896,512]{1,0:T(8,128)S(1)} %get-tuple-element.131, f32[5,512]{1,0:T(8,128)S(1)} %broadcast_multiply_fusion, f32[512]{0:T(512)S(1)} %mul.154, f32[512]{0:T(512)S(1)} %mul.149, f32[512]{0:T(512)S(1)} %sub.53, f32[896]{0:T(1024)S(1)} %iota_add_fusion, ...), kind=kOutput, calls=%fused_computation.2 | convolution fusion | flops 4162024960 | bytes 11728384 | tf_op jit(solution)/shard_map/bij,js->bis/dot_general | solution.py:100
  227.7 2.2 multiply_reduce_fusion.6
  231.2 21.9 %all_to_all.18 = f32[8,128,4]{0,2,1:T(4,128)S(1)} all-to-all(f32[8,128,4]{0,2,1:T(4,128)S(1)} %copy.98), channel_id=1, replica_groups=mesh['ra'=16,'dec'=8] {'ra','dec'}, dimensions={1} | all-to-all | bytes 32768 | tf_op jit(solution)/shard_map/all_to_all | solution.py:117
  (82 shorter events, 25.2 us)
Async XLA Ops:
  3.8 23.8 %all-to-all-start = ((f32[9,128,4]{0,2,1:T(4,128)}), f32[9,128,4]{0,2,1:T(4,128)S(1)}, u32[]{:S(2)}, u32[]{:S(2)}) async-start(f32[9,128,4]{0,2,1:T(4,128)} %bitcast.4), calls=%async_computation | async-start | bytes 524288 | tf_op jit(solution)/shard_map/all_to_all | solution.py:61
  36.1 15.6 %collective-permute-start.5 = (bf16[5,128,256]{1,2,0:T(8,128)(2,1)S(1)}, bf16[5,128,256]{1,2,0:T(8,128)(2,1)S(1)}, u32[]{:S(2)}, u32[]{:S(2)}) collective-permute-start(bf16[5,128,256]{1,2,0:T(8,128)(2,1)S(1)} %pad_maximum_fusion.5), channel_id=1, source_target_pairs={{0,8},{8,16},{16,24},{24,32},{32,40},{40,48},{48,56},{56,64},{64,7... | collective-permute-start | bytes 983048 | tf_op jit(solution)/shard_map/ppermute | solution.py:14
  41.2 10.5 %collective-permute-start.4 = (bf16[5,128,256]{1,2,0:T(8,128)(2,1)S(1)}, bf16[5,128,256]{1,2,0:T(8,128)(2,1)S(1)}, u32[]{:S(2)}, u32[]{:S(2)}) collective-permute-start(bf16[5,128,256]{1,2,0:T(8,128)(2,1)S(1)} %pad_maximum_fusion.4), channel_id=1, source_target_pairs={{8,0},{16,8},{24,16},{32,24},{40,32},{48,40},{56,48},{64,56},{72,6... | collective-permute-start | bytes 983048 | tf_op jit(solution)/shard_map/ppermute | solution.py:14
  43.3 62.5 %collective-permute-start.1 = (bf16[5,128,640]{1,2,0:T(8,128)(2,1)S(1)}, bf16[5,128,640]{1,2,0:T(8,128)(2,1)S(1)}, u32[]{:S(2)}, u32[]{:S(2)}) collective-permute-start(bf16[5,128,640]{1,2,0:T(8,128)(2,1)S(1)} %get-tuple-element.120), channel_id=1, source_target_pairs={{0,8},{8,16},{16,24},{24,32},{32,40},{40,48},{48,56},{56,64},{64,7... | collective-permute-start | bytes 2457608 | tf_op jit(solution)/shard_map/ppermute | solution.py:14
  48.5 57.0 %collective-permute-start = (bf16[5,128,640]{1,2,0:T(8,128)(2,1)S(1)}, bf16[5,128,640]{1,2,0:T(8,128)(2,1)S(1)}, u32[]{:S(2)}, u32[]{:S(2)}) collective-permute-start(bf16[5,128,640]{1,2,0:T(8,128)(2,1)S(1)} %get-tuple-element.121), channel_id=1, source_target_pairs={{8,0},{16,8},{24,16},{32,24},{40,32},{48,40},{56,48},{64,56},{72,6... | collective-permute-start | bytes 2457608 | tf_op jit(solution)/shard_map/ppermute | solution.py:14
  50.4 55.8 %collective-permute-start.2 = (bf16[5,640,128]{1,2,0:T(8,128)(2,1)S(1)}, bf16[5,640,128]{1,2,0:T(8,128)(2,1)S(1)}, u32[]{:S(2)}, u32[]{:S(2)}) collective-permute-start(bf16[5,640,128]{1,2,0:T(8,128)(2,1)S(1)} %get-tuple-element.119), channel_id=1, source_target_pairs={{1,0},{2,1},{3,2},{4,3},{5,4},{6,5},{7,6},{9,8},{10,9},{11,10},{12... | collective-permute-start | bytes 2457608 | tf_op jit(solution)/shard_map/ppermute | solution.py:14
  51.9 50.0 %collective-permute-start.6 = (bf16[5,256,128]{1,2,0:T(8,128)(2,1)S(1)}, bf16[5,256,128]{1,2,0:T(8,128)(2,1)S(1)}, u32[]{:S(2)}, u32[]{:S(2)}) collective-permute-start(bf16[5,256,128]{1,2,0:T(8,128)(2,1)S(1)} %pad_maximum_fusion.6), channel_id=1, source_target_pairs={{1,0},{2,1},{3,2},{4,3},{5,4},{6,5},{7,6},{9,8},{10,9},{11,10},{12... | collective-permute-start | bytes 983048 | tf_op jit(solution)/shard_map/ppermute | solution.py:14
  53.2 52.3 %collective-permute-start.7 = (bf16[5,256,128]{1,2,0:T(8,128)(2,1)S(1)}, bf16[5,256,128]{1,2,0:T(8,128)(2,1)S(1)}, u32[]{:S(2)}, u32[]{:S(2)}) collective-permute-start(bf16[5,256,128]{1,2,0:T(8,128)(2,1)S(1)} %pad_maximum_fusion.7), channel_id=1, source_target_pairs={{0,1},{1,2},{2,3},{3,4},{4,5},{5,6},{6,7},{8,9},{9,10},{10,11},{11... | collective-permute-start | bytes 983048 | tf_op jit(solution)/shard_map/ppermute | solution.py:14
  101.8 12.6 %collective-permute-start.3 = (bf16[5,640,128]{1,2,0:T(8,128)(2,1)S(1)}, bf16[5,640,128]{1,2,0:T(8,128)(2,1)S(1)}, u32[]{:S(2)}, u32[]{:S(2)}) collective-permute-start(bf16[5,640,128]{1,2,0:T(8,128)(2,1)S(1)} %get-tuple-element.118), channel_id=1, source_target_pairs={{0,1},{1,2},{2,3},{3,4},{4,5},{5,6},{6,7},{8,9},{9,10},{10,11},{11... | collective-permute-start | bytes 2457608 | tf_op jit(solution)/shard_map/ppermute | solution.py:14
  114.9 3.2 %copy-start = (f32[5,640,640]{1,2,0:T(8,128)}, f32[5,640,640]{1,2,0:T(8,128)S(1)}, u32[]{:S(2)}) copy-start(f32[5,640,640]{1,2,0:T(8,128)S(1)} %fusion.24) | copy-start | bytes 24576004
  114.9 14.7 %copy-start.7 = (f32[1,1,5]{2,1,0:T(1,128)S(1)}, f32[1,1,5]{2,1,0:T(1,128)}, u32[]{:S(2)}) copy-start(f32[1,1,5]{2,1,0:T(1,128)} %param.26) | copy-start | bytes 64
  136.8 27.3 %copy-start.1 = (bf16[5,640,640]{1,2,0:T(8,128)(2,1)}, bf16[5,640,640]{1,2,0:T(8,128)(2,1)S(1)}, u32[]{:S(2)}) copy-start(bf16[5,640,640]{1,2,0:T(8,128)(2,1)S(1)} %add_convert_fusion) | copy-start | bytes 12288004
  137.1 25.1 %collective-permute-start.8 = (bf16[5,128,640]{1,2,0:T(8,128)(2,1)S(1)}, bf16[5,128,640]{1,2,0:T(8,128)(2,1)S(1)}, u32[]{:S(2)}, u32[]{:S(2)}) collective-permute-start(bf16[5,128,640]{1,2,0:T(8,128)(2,1)S(1)} %get-tuple-element.124), channel_id=1, source_target_pairs={{0,8},{8,16},{16,24},{24,32},{32,40},{40,48},{48,56},{56,64},{64,7... | collective-permute-start | bytes 2457608 | tf_op jit(solution)/shard_map/ppermute | solution.py:25
  139.1 23.2 %collective-permute-start.9 = (bf16[5,128,640]{1,2,0:T(8,128)(2,1)S(1)}, bf16[5,128,640]{1,2,0:T(8,128)(2,1)S(1)}, u32[]{:S(2)}, u32[]{:S(2)}) collective-permute-start(bf16[5,128,640]{1,2,0:T(8,128)(2,1)S(1)} %get-tuple-element.125), channel_id=1, source_target_pairs={{8,0},{16,8},{24,16},{32,24},{40,32},{48,40},{56,48},{64,56},{72,6... | collective-permute-start | bytes 2457608 | tf_op jit(solution)/shard_map/ppermute | solution.py:27
  162.2 1.9 copy-start.3
  162.2 1.9 copy-start.5
  164.2 18.2 %collective-permute-start.10 = (bf16[5,896,128]{1,2,0:T(8,128)(2,1)}, bf16[5,896,128]{1,2,0:T(8,128)(2,1)}, u32[]{:S(2)}, u32[]{:S(2)}) collective-permute-start(bf16[5,896,128]{1,2,0:T(8,128)(2,1)} %get-tuple-element.122), channel_id=1, source_target_pairs={{0,1},{1,2},{2,3},{3,4},{4,5},{5,6},{6,7},{8,9},{9,10},{10,11},{11... | collective-permute-start | bytes 3440648 | tf_op jit(solution)/shard_map/ppermute | solution.py:25
  170.3 39.8 %collective-permute-start.11 = (bf16[5,896,128]{1,2,0:T(8,128)(2,1)}, bf16[5,896,128]{1,2,0:T(8,128)(2,1)}, u32[]{:S(2)}, u32[]{:S(2)}) collective-permute-start(bf16[5,896,128]{1,2,0:T(8,128)(2,1)} %get-tuple-element.123), channel_id=1, source_target_pairs={{1,0},{2,1},{3,2},{4,3},{5,4},{6,5},{7,6},{9,8},{10,9},{11,10},{12... | collective-permute-start | bytes 3440648 | tf_op jit(solution)/shard_map/ppermute | solution.py:27
  171.7 48.3 %copy-start.2 = (bf16[5,640,640]{1,2,0:T(8,128)(2,1)S(1)}, bf16[5,640,640]{1,2,0:T(8,128)(2,1)}, u32[]{:S(2)}) copy-start(bf16[5,640,640]{1,2,0:T(8,128)(2,1)} %copy-done.1) | copy-start | bytes 12288004
  171.7 48.3 %copy-start.4 = (bf16[5,128,640]{1,2,0:T(8,128)(2,1)S(1)}, bf16[5,128,640]{1,2,0:T(8,128)(2,1)}, u32[]{:S(2)}) copy-start(bf16[5,128,640]{1,2,0:T(8,128)(2,1)} %copy-done.3) | copy-start | bytes 2457604
  171.7 48.3 %copy-start.6 = (bf16[5,128,640]{1,2,0:T(8,128)(2,1)S(1)}, bf16[5,128,640]{1,2,0:T(8,128)(2,1)}, u32[]{:S(2)}) copy-start(bf16[5,128,640]{1,2,0:T(8,128)(2,1)} %copy-done.5) | copy-start | bytes 2457604
where the time goes:
time: 255 us; the launch traced here: 254 us
  waiting for transfers between devices  110 us (43%)
  starting transfers between devices  48.1 us (19%)
  matrix products  25.9 us (10%)
  other arithmetic  24.2 us (9%)
  local copies, waits for them, and re-layouts  23.2 us (9%)
  blocking collectives  21.9 us (9%)
    ppermute x8, waiting for transfers between devices, passed_along(): lax.ppermute(value, axis, [(source, source + steps) for source in range(l...  51.3 us
    ppermute x2, waiting for transfers between devices, with_halo(): lax.ppermute(tail, axis, [(i, (i + 1) % count) for i in range(ends)])  31.4 us
    ppermute x2, waiting for transfers between devices, with_halo(): lax.ppermute(head, axis, [((i + 1) % count, i) for i in range(ends)])  27.7 us
    ppermute x8, starting transfers between devices, passed_along(): lax.ppermute(value, axis, [(source, source + steps) for source in range(l...  24.8 us
    all_to_all x1, blocking collectives, on_device(): lax.all_to_all(slot_grad, ('ra', 'dec'), split_axis=1, concat_axis=1, til...  21.9 us
    unnamed x18, local copies, waits for them, and re-layouts  13.6 us
    all_to_all x1, starting transfers between devices, on_device(): lax.all_to_all(outgoing, ('ra', 'dec'), split_axis=1, concat_axis=1, tile...  11.5 us
    dot_general x1, matrix products, on_device(): jnp.einsum('bij,is->bjs', weight_canvas, row_bf, preferred_element_type=j...  9.9 us
  transfers between devices with their start and end apart: 13, of which 5 were waited for; matrix products, arithmetic and copies ran while one was open for 6% of the time, Pallas kernels for 0%

commit v1 on v0

--- a/solution.py
+++ b/solution.py
@@ -1,3 +1,4 @@
+import functools
 import math
 import jax
 import jax.numpy as jnp
@@ -6,6 +7,17 @@
 
 MARGIN = 128
 CAT_DEV = 256
+
+
+def apply_lane_over_axis(frame_in, axis_tag):
+    seen_now = jax.lax.axis_size(axis_tag)
+    out_arr = jnp.split(frame_in, seen_now, 1)
+    shaped = jnp.stack(out_arr, 0)
+    e_next = jax.lax.all_to_all(shaped, axis_tag, 0, 0)
+    return jnp.concatenate(e_next, 1)
+
+
+sums_all_supply_all = functools.partial(apply_lane_over_axis, axis_tag=("ra", "dec"))
 
 
 def passed_along(value, axis, steps):
@@ -58,7 +70,7 @@
         [log_flux, position, log_width[None, :], jnp.ones((1, rows_here), jnp.float32)], axis=0
     )
     outgoing = jnp.dot(params, onehot, precision=lax.Precision.HIGHEST)
-    arrived = lax.all_to_all(outgoing, ("ra", "dec"), split_axis=1, concat_axis=1, tiled=True)
+    arrived = sums_all_supply_all(outgoing)
     flux_values = arrived[8][None, :] * jnp.exp(arrived[0:5])
     row_prof, row_off, sigma = profiles(arrived[5], arrived[7], canvas_side)
     col_prof, col_off, _ = profiles(arrived[6], arrived[7], canvas_side)

time: 255 us -> 334 us (1.31)
  local copies, waits for them, and re-layouts: 23.2 us -> 110 us
  matrix products: 25.9 us -> 20.1 us
  waiting for transfers between devices: 110 us -> 115 us
    unnamed x18 -> x138, local copies, waits for them, and re-layouts: 13.6 us -> 86.9 us
    split x0 -> x135, local copies, waits for them, and re-layouts: none -> 12.3 us  [apply_lane_over_axis(): out_arr = jnp.split(frame_in, seen_now, 1)]
    dot_general x1, matrix products: 9.9 us -> 5.23 us  [on_device(): jnp.einsum('bij,is->bjs', weight_canvas, row_bf, preferred_element_type=j...]
    ppermute x2, waiting for transfers between devices: 31.4 us -> 35 us  [with_halo(): lax.ppermute(tail, axis, [(i, (i + 1) % count) for i in range(ends)])]
  transfers between devices with their start and end apart: 13 -> 13, of which waited for: 5 -> 5; matrix products, arithmetic and copies ran while one was open for 6% -> 4% of each run, Pallas kernels for 0% -> 0%
where the time goes in v1:
time: 334 us; the launch traced here: 333 us
  waiting for transfers between devices  115 us (34%)
  local copies, waits for them, and re-layouts  110 us (33%)
  starting transfers between devices  45.5 us (14%)
  blocking collectives  21.1 us (6%)
  other arithmetic  20.9 us (6%)
  matrix products  20.1 us (6%)
    unnamed x138, local copies, waits for them, and re-layouts  86.9 us
    ppermute x8, waiting for transfers between devices, passed_along(): lax.ppermute(value, axis, [(source, source + steps) for source in range(l...  51.3 us
    ppermute x2, waiting for transfers between devices, with_halo(): lax.ppermute(tail, axis, [(i, (i + 1) % count) for i in range(ends)])  35 us
    ppermute x2, waiting for transfers between devices, with_halo(): lax.ppermute(head, axis, [((i + 1) % count, i) for i in range(ends)])  28.3 us
    ppermute x8, starting transfers between devices, passed_along(): lax.ppermute(value, axis, [(source, source + steps) for source in range(l...  24.8 us
    all_to_all x1, blocking collectives, on_device(): lax.all_to_all(slot_grad, ('ra', 'dec'), split_axis=1, concat_axis=1, til...  21.1 us
    split x135, local copies, waits for them, and re-layouts, apply_lane_over_axis(): out_arr = jnp.split(frame_in, seen_now, 1)  12.3 us
    all_to_all x1, starting transfers between devices, apply_lane_over_axis(): e_next = jax.lax.all_to_all(shaped, axis_tag, 0, 0)  11.5 us
  transfers between devices with their start and end apart: 13, of which 5 were waited for; matrix products, arithmetic and copies ran while one was open for 4% of the time, Pallas kernels for 0%

profile of v1, /device:TPU:1, one launch (start us, length us, event | category | flops | bytes accessed | tf_op | source)
XLA Modules:
  0.0 333.5 jit_solution(16713871122803871856)
XLA Ops:
  89.3 11.5 %all-to-all-start = ((f32[128,9,4]{1,2,0:T(4,128)}), f32[128,9,4]{1,2,0:T(4,128)S(1)}, u32[]{:S(2)}, u32[]{:S(2)}) async-start(f32[128,9,4]{1,2,0:T(4,128)} %constant_dynamic-update-slice_fusion), calls=%async_computation | async-start | bytes 524288 | tf_op jit(solution)/shard_map/all_to_all | solution.py:16
  102.1 10.3 %copy.1206 = s32[5,640,640]{1,2,0:T(8,128)} copy(s32[5,640,640]{2,1,0:T(8,128)} %param.27) | data formatting | bytes 16384000 | tf_op args[5]
  114.7 5.1 %convolution_convert_fusion = bf16[5,896,896]{1,2,0:T(8,128)(2,1)S(1)} fusion(f32[5,512]{1,0:T(8,128)S(1)} %broadcast_multiply_fusion, f32[896,512]{1,0:T(8,128)S(1)} %get-tuple-element.260, f32[512]{0:T(512)S(1)} %mul.158, f32[512]{0:T(512)S(1)} %mul.153, f32[512]{0:T(512)S(1)} %sub.53, f32[896]{0:T(1024)S(1)} %iota_add_fusion), kind=kOutput, calls=%fused_computation.6 | convolution fusion | flops 4121772032 | bytes 9883136 | tf_op jit(solution)/shard_map/bis,js->bij/dot_general | solution.py:80
  120.4 5.1 %collective-permute-start.5 = (bf16[5,128,256]{1,2,0:T(8,128)(2,1)S(1)}, bf16[5,128,256]{1,2,0:T(8,128)(2,1)S(1)}, u32[]{:S(2)}, u32[]{:S(2)}) collective-permute-start(bf16[5,128,256]{1,2,0:T(8,128)(2,1)S(1)} %pad_maximum_fusion.6), channel_id=1, source_target_pairs={{0,8},{8,16},{16,24},{24,32},{32,40},{40,48},{48,56},{56,64},{64,7... | collective-permute-start | bytes 983048 | tf_op jit(solution)/shard_map/ppermute | solution.py:26
  125.5 1.9 collective-permute-start.4
  127.6 5.1 %collective-permute-start.1 = (bf16[5,128,640]{1,2,0:T(8,128)(2,1)S(1)}, bf16[5,128,640]{1,2,0:T(8,128)(2,1)S(1)}, u32[]{:S(2)}, u32[]{:S(2)}) collective-permute-start(bf16[5,128,640]{1,2,0:T(8,128)(2,1)S(1)} %get-tuple-element.115), channel_id=1, source_target_pairs={{0,8},{8,16},{16,24},{24,32},{32,40},{40,48},{48,56},{56,64},{64,7... | collective-permute-start | bytes 2457608 | tf_op jit(solution)/shard_map/ppermute | solution.py:26
  132.7 1.9 collective-permute-start
  137.4 4.6 %collective-permute-start.7 = (bf16[5,256,128]{1,2,0:T(8,128)(2,1)S(1)}, bf16[5,256,128]{1,2,0:T(8,128)(2,1)S(1)}, u32[]{:S(2)}, u32[]{:S(2)}) collective-permute-start(bf16[5,256,128]{1,2,0:T(8,128)(2,1)S(1)} %pad_maximum_fusion.8), channel_id=1, source_target_pairs={{0,1},{1,2},{2,3},{3,4},{4,5},{5,6},{6,7},{8,9},{9,10},{10,11},{11... | collective-permute-start | bytes 983048 | tf_op jit(solution)/shard_map/ppermute | solution.py:26
  142.6 43.4 %collective-permute-done.6 = bf16[5,256,128]{1,2,0:T(8,128)(2,1)S(1)} collective-permute-done((bf16[5,256,128]{1,2,0:T(8,128)(2,1)S(1)}, bf16[5,256,128]{1,2,0:T(8,128)(2,1)S(1)}, u32[]{:S(2)}, u32[]{:S(2)}) %collective-permute-start.6) | collective-permute-done | bytes 327712 | tf_op jit(solution)/shard_map/ppermute | solution.py:26
  186.0 3.6 %collective-permute-start.3 = (bf16[5,640,128]{1,2,0:T(8,128)(2,1)S(1)}, bf16[5,640,128]{1,2,0:T(8,128)(2,1)S(1)}, u32[]{:S(2)}, u32[]{:S(2)}) collective-permute-start(bf16[5,640,128]{1,2,0:T(8,128)(2,1)S(1)} %get-tuple-element.113), channel_id=1, source_target_pairs={{0,1},{1,2},{2,3},{3,4},{4,5},{5,6},{6,7},{8,9},{9,10},{10,11},{11... | collective-permute-start | bytes 2457608 | tf_op jit(solution)/shard_map/ppermute | solution.py:26
  190.8 7.9 %collective-permute-done.3 = bf16[5,640,128]{1,2,0:T(8,128)(2,1)S(1)} collective-permute-done((bf16[5,640,128]{1,2,0:T(8,128)(2,1)S(1)}, bf16[5,640,128]{1,2,0:T(8,128)(2,1)S(1)}, u32[]{:S(2)}, u32[]{:S(2)}) %collective-permute-start.3) | collective-permute-done | bytes 819232 | tf_op jit(solution)/shard_map/ppermute | solution.py:26
  199.1 3.1 copy-done
  202.3 2.1 add_select_fusion
  204.4 5.8 %scatter-add.35 = f32[5,640,640]{1,2,0:T(8,128)} dynamic-update-slice(f32[5,640,640]{1,2,0:T(8,128)} %copy-done, f32[5,128,128]{1,2,0:T(8,128)S(1)} %add_select_fusion, s32[]{:T(128)} %constant.235.clone.1, s32[]{:T(128)} %bitcast.136, s32[]{:T(128)} %bitcast.137) | dynamic-update-slice | bytes 655364 | tf_op jit(solution)/shard_map/scatter-add | solution.py:106
  213.8 7.3 %add_convert_fusion = bf16[5,640,640]{1,2,0:T(8,128)(2,1)S(1)} fusion(f32[5,640,640]{1,2,0:T(8,128)} %fusion.22, s32[5,640,640]{1,2,0:T(8,128)} %copy.1206, f32[5]{0:T(128)S(1)} %bitcast.287), kind=kLoop, calls=%fused_computation.4 | loop fusion | flops 10240000 | bytes 20480020 | tf_op jit(solution)/shard_map/convert_element_type | solution.py:110
  223.4 2.5 collective-permute-start.9
  225.8 22.4 %collective-permute-done.8 = bf16[5,128,640]{1,2,0:T(8,128)(2,1)S(1)} collective-permute-done((bf16[5,128,640]{1,2,0:T(8,128)(2,1)S(1)}, bf16[5,128,640]{1,2,0:T(8,128)(2,1)S(1)}, u32[]{:S(2)}, u32[]{:S(2)}) %collective-permute-start.8) | collective-permute-done | bytes 819232 | tf_op jit(solution)/shard_map/ppermute | solution.py:37
  248.5 3.5 %collective-permute-start.10 = (bf16[5,896,128]{1,2,0:T(8,128)(2,1)S(1)}, bf16[5,896,128]{1,2,0:T(8,128)(2,1)S(1)}, u32[]{:S(2)}, u32[]{:S(2)}) collective-permute-start(bf16[5,896,128]{1,2,0:T(8,128)(2,1)S(1)} %get-tuple-element.117), channel_id=1, source_target_pairs={{0,1},{1,2},{2,3},{3,4},{4,5},{5,6},{6,7},{8,9},{9,10},{10,11},{11... | collective-permute-start | bytes 3440648 | tf_op jit(solution)/shard_map/ppermute | solution.py:37
  253.3 12.7 %collective-permute-done.10 = bf16[5,896,128]{1,2,0:T(8,128)(2,1)S(1)} collective-permute-done((bf16[5,896,128]{1,2,0:T(8,128)(2,1)S(1)}, bf16[5,896,128]{1,2,0:T(8,128)(2,1)S(1)}, u32[]{:S(2)}, u32[]{:S(2)}) %collective-permute-start.10) | collective-permute-done | bytes 1146912 | tf_op jit(solution)/shard_map/ppermute | solution.py:37
  266.0 28.3 %collective-permute-done.11 = bf16[5,896,128]{1,2,0:T(8,128)(2,1)S(1)} collective-permute-done((bf16[5,896,128]{1,2,0:T(8,128)(2,1)S(1)}, bf16[5,896,128]{1,2,0:T(8,128)(2,1)S(1)}, u32[]{:S(2)}, u32[]{:S(2)}) %collective-permute-start.11) | collective-permute-done | bytes 1146912 | tf_op jit(solution)/shard_map/ppermute | solution.py:39
  294.3 5.2 %multiply_reduce_fusion = f32[896,512]{1,0:T(8,128)S(1)} fusion(f32[5,512]{1,0:T(8,128)S(1)} %broadcast_multiply_fusion, f32[512]{0:T(512)S(1)} %mul.158, f32[512]{0:T(512)S(1)} %mul.153, f32[512]{0:T(512)S(1)} %sub.50, f32[896]{0:T(1024)S(1)} %iota_add_fusion, bf16[5,896,128]{1,2,0:T(8,128)(2,1)S(1)} %collective-permute-done.11, ...), kind=kOutput, calls=%fused_computation | convolution fusion | flops 4157440000 | bytes 9883136 | tf_op jit(solution)/shard_map/bij,is->bjs/dot_general | solution.py:115
  299.5 7.7 %multiply_reduce_fusion.2 = (f32[5,512]{1,0:T(8,128)S(1)}, f32[896,512]{1,0:T(8,128)S(1)}) fusion(f32[896,512]{1,0:T(8,128)S(1)} %get-tuple-element.259, f32[5,512]{1,0:T(8,128)S(1)} %broadcast_multiply_fusion, f32[512]{0:T(512)S(1)} %mul.158, f32[512]{0:T(512)S(1)} %mul.153, f32[512]{0:T(512)S(1)} %sub.53, f32[896]{0:T(1024)S(1)} %iota_add_fusion, ...), kind=kOutput, calls=%fused_computation.2 | convolution fusion | flops 4162024960 | bytes 11728384 | tf_op jit(solution)/shard_map/bij,js->bis/dot_general | solution.py:112
  307.2 2.5 multiply_reduce_fusion.6
  311.4 21.1 %all_to_all.14 = f32[8,128,4]{0,2,1:T(4,128)S(1)} all-to-all(f32[8,128,4]{0,2,1:T(4,128)S(1)} %copy.1208), channel_id=1, replica_groups=mesh['ra'=16,'dec'=8] {'ra','dec'}, dimensions={1} | all-to-all | bytes 32768 | tf_op jit(solution)/shard_map/all_to_all | solution.py:129
  (333 shorter events, 108.3 us)
Async XLA Ops:
  3.2 98.2 %copy-start.2 = (s32[3]{0:T(128)S(1)}, s32[3]{0:T(128)}, u32[]{:S(2)}) copy-start(s32[3]{0:T(128)} %constant.242.clone.1) | copy-start | bytes 40
  89.3 23.1 %all-to-all-start = ((f32[128,9,4]{1,2,0:T(4,128)}), f32[128,9,4]{1,2,0:T(4,128)S(1)}, u32[]{:S(2)}, u32[]{:S(2)}) async-start(f32[128,9,4]{1,2,0:T(4,128)} %constant_dynamic-update-slice_fusion), calls=%async_computation | async-start | bytes 524288 | tf_op jit(solution)/shard_map/all_to_all | solution.py:16
  120.4 15.6 %collective-permute-start.5 = (bf16[5,128,256]{1,2,0:T(8,128)(2,1)S(1)}, bf16[5,128,256]{1,2,0:T(8,128)(2,1)S(1)}, u32[]{:S(2)}, u32[]{:S(2)}) collective-permute-start(bf16[5,128,256]{1,2,0:T(8,128)(2,1)S(1)} %pad_maximum_fusion.6), channel_id=1, source_target_pairs={{0,8},{8,16},{16,24},{24,32},{32,40},{40,48},{48,56},{56,64},{64,7... | collective-permute-start | bytes 983048 | tf_op jit(solution)/shard_map/ppermute | solution.py:26
  125.5 10.5 %collective-permute-start.4 = (bf16[5,128,256]{1,2,0:T(8,128)(2,1)S(1)}, bf16[5,128,256]{1,2,0:T(8,128)(2,1)S(1)}, u32[]{:S(2)}, u32[]{:S(2)}) collective-permute-start(bf16[5,128,256]{1,2,0:T(8,128)(2,1)S(1)} %pad_maximum_fusion.5), channel_id=1, source_target_pairs={{8,0},{16,8},{24,16},{32,24},{40,32},{48,40},{56,48},{64,56},{72,6... | collective-permute-start | bytes 983048 | tf_op jit(solution)/shard_map/ppermute | solution.py:26
  127.6 62.5 %collective-permute-start.1 = (bf16[5,128,640]{1,2,0:T(8,128)(2,1)S(1)}, bf16[5,128,640]{1,2,0:T(8,128)(2,1)S(1)}, u32[]{:S(2)}, u32[]{:S(2)}) collective-permute-start(bf16[5,128,640]{1,2,0:T(8,128)(2,1)S(1)} %get-tuple-element.115), channel_id=1, source_target_pairs={{0,8},{8,16},{16,24},{24,32},{32,40},{40,48},{48,56},{56,64},{64,7... | collective-permute-start | bytes 2457608 | tf_op jit(solution)/shard_map/ppermute | solution.py:26
  132.7 57.0 %collective-permute-start = (bf16[5,128,640]{1,2,0:T(8,128)(2,1)S(1)}, bf16[5,128,640]{1,2,0:T(8,128)(2,1)S(1)}, u32[]{:S(2)}, u32[]{:S(2)}) collective-permute-start(bf16[5,128,640]{1,2,0:T(8,128)(2,1)S(1)} %get-tuple-element.116), channel_id=1, source_target_pairs={{8,0},{16,8},{24,16},{32,24},{40,32},{48,40},{56,48},{64,56},{72,6... | collective-permute-start | bytes 2457608 | tf_op jit(solution)/shard_map/ppermute | solution.py:26
  134.6 55.8 %collective-permute-start.2 = (bf16[5,640,128]{1,2,0:T(8,128)(2,1)S(1)}, bf16[5,640,128]{1,2,0:T(8,128)(2,1)S(1)}, u32[]{:S(2)}, u32[]{:S(2)}) collective-permute-start(bf16[5,640,128]{1,2,0:T(8,128)(2,1)S(1)} %get-tuple-element.114), channel_id=1, source_target_pairs={{1,0},{2,1},{3,2},{4,3},{5,4},{6,5},{7,6},{9,8},{10,9},{11,10},{12... | collective-permute-start | bytes 2457608 | tf_op jit(solution)/shard_map/ppermute | solution.py:26
  136.1 50.0 %collective-permute-start.6 = (bf16[5,256,128]{1,2,0:T(8,128)(2,1)S(1)}, bf16[5,256,128]{1,2,0:T(8,128)(2,1)S(1)}, u32[]{:S(2)}, u32[]{:S(2)}) collective-permute-start(bf16[5,256,128]{1,2,0:T(8,128)(2,1)S(1)} %pad_maximum_fusion.7), channel_id=1, source_target_pairs={{1,0},{2,1},{3,2},{4,3},{5,4},{6,5},{7,6},{9,8},{10,9},{11,10},{12... | collective-permute-start | bytes 983048 | tf_op jit(solution)/shard_map/ppermute | solution.py:26
  137.4 52.3 %collective-permute-start.7 = (bf16[5,256,128]{1,2,0:T(8,128)(2,1)S(1)}, bf16[5,256,128]{1,2,0:T(8,128)(2,1)S(1)}, u32[]{:S(2)}, u32[]{:S(2)}) collective-permute-start(bf16[5,256,128]{1,2,0:T(8,128)(2,1)S(1)} %pad_maximum_fusion.8), channel_id=1, source_target_pairs={{0,1},{1,2},{2,3},{3,4},{4,5},{5,6},{6,7},{8,9},{9,10},{10,11},{11... | collective-permute-start | bytes 983048 | tf_op jit(solution)/shard_map/ppermute | solution.py:26
  186.0 12.6 %collective-permute-start.3 = (bf16[5,640,128]{1,2,0:T(8,128)(2,1)S(1)}, bf16[5,640,128]{1,2,0:T(8,128)(2,1)S(1)}, u32[]{:S(2)}, u32[]{:S(2)}) collective-permute-start(bf16[5,640,128]{1,2,0:T(8,128)(2,1)S(1)} %get-tuple-element.113), channel_id=1, source_target_pairs={{0,1},{1,2},{2,3},{3,4},{4,5},{5,6},{6,7},{8,9},{9,10},{10,11},{11... | collective-permute-start | bytes 2457608 | tf_op jit(solution)/shard_map/ppermute | solution.py:26
  199.1 3.2 copy-start
  199.1 14.7 %copy-start.1 = (f32[1,1,5]{2,1,0:T(1,128)S(1)}, f32[1,1,5]{2,1,0:T(1,128)}, u32[]{:S(2)}) copy-start(f32[1,1,5]{2,1,0:T(1,128)} %param.26) | copy-start | bytes 64
  221.4 26.7 %collective-permute-start.8 = (bf16[5,128,640]{1,2,0:T(8,128)(2,1)S(1)}, bf16[5,128,640]{1,2,0:T(8,128)(2,1)S(1)}, u32[]{:S(2)}, u32[]{:S(2)}) collective-permute-start(bf16[5,128,640]{1,2,0:T(8,128)(2,1)S(1)} %get-tuple-element.119), channel_id=1, source_target_pairs={{0,8},{8,16},{16,24},{24,32},{32,40},{40,48},{48,56},{56,64},{64,7... | collective-permute-start | bytes 2457608 | tf_op jit(solution)/shard_map/ppermute | solution.py:37
  223.4 24.8 %collective-permute-start.9 = (bf16[5,128,640]{1,2,0:T(8,128)(2,1)S(1)}, bf16[5,128,640]{1,2,0:T(8,128)(2,1)S(1)}, u32[]{:S(2)}, u32[]{:S(2)}) collective-permute-start(bf16[5,128,640]{1,2,0:T(8,128)(2,1)S(1)} %get-tuple-element.120), channel_id=1, source_target_pairs={{8,0},{16,8},{24,16},{32,24},{40,32},{48,40},{56,48},{64,56},{72,6... | collective-permute-start | bytes 2457608 | tf_op jit(solution)/shard_map/ppermute | solution.py:39
  248.5 17.5 %collective-permute-start.10 = (bf16[5,896,128]{1,2,0:T(8,128)(2,1)S(1)}, bf16[5,896,128]{1,2,0:T(8,128)(2,1)S(1)}, u32[]{:S(2)}, u32[]{:S(2)}) collective-permute-start(bf16[5,896,128]{1,2,0:T(8,128)(2,1)S(1)} %get-tuple-element.117), channel_id=1, source_target_pairs={{0,1},{1,2},{2,3},{3,4},{4,5},{5,6},{6,7},{8,9},{9,10},{10,11},{11... | collective-permute-start | bytes 3440648 | tf_op jit(solution)/shard_map/ppermute | solution.py:37
  252.0 42.2 %collective-permute-start.11 = (bf16[5,896,128]{1,2,0:T(8,128)(2,1)S(1)}, bf16[5,896,128]{1,2,0:T(8,128)(2,1)S(1)}, u32[]{:S(2)}, u32[]{:S(2)}) collective-permute-start(bf16[5,896,128]{1,2,0:T(8,128)(2,1)S(1)} %get-tuple-element.118), channel_id=1, source_target_pairs={{1,0},{2,1},{3,2},{4,3},{5,4},{6,5},{7,6},{9,8},{10,9},{11,10},{12... | collective-permute-start | bytes 3440648 | tf_op jit(solution)/shard_map/ppermute | solution.py:39
  266.0 33.5 %copy-start.3 = (bf16[5,896,128]{1,2,0:T(8,128)(2,1)}, bf16[5,896,128]{1,2,0:T(8,128)(2,1)S(1)}, u32[]{:S(2)}) copy-start(bf16[5,896,128]{1,2,0:T(8,128)(2,1)S(1)} %collective-permute-done.10) | copy-start | bytes 3440644
  294.2 5.2 %copy-start.4 = (bf16[5,896,128]{1,2,0:T(8,128)(2,1)}, bf16[5,896,128]{1,2,0:T(8,128)(2,1)S(1)}, u32[]{:S(2)}) copy-start(bf16[5,896,128]{1,2,0:T(8,128)(2,1)S(1)} %collective-permute-done.11) | copy-start | bytes 3440644
